TPU v7x, 128 devices: a whole 4x4x4 slice. The times are simulated.
128 devices in a mesh: row: 8 (over z, core), col: 16 (over x, y).
Axes of the slice: x: 4, y: 4, z: 4, core: 2. Of those that a mesh axis runs over, the one named last changes fastest.
Arguments:
- hessian_inverse: float32 [12288, 12288], P('row', 'col'), as said below
- weight: bfloat16 [12288, 4096], P('row', 'col'), may hold values from -6 to 6
- pruned: int32 [2, 512], replicated, may hold values from 0 to 12287, as said below
Outputs:
- hessian_after: float32 [12288, 12288], P('row', 'col')
- weight_after: bfloat16 [12288, 4096], P('row', 'col')
Inputs may be any that keep to these rules, and one draw needn't show every extreme that they name: `hessian_inverse`: symmetric and positive definite. `pruned`: all 1024 channel numbers are distinct.
All inputs are finite; a program needn't handle non-finite values.
Results may differ from a plain program's by a relative error of at most 0.001.
Values sent between devices are 32-bit elements; how exact they have to be, the bound alone decides.
No kernel may reach another device: no remote copies, remote signals or barrier semaphores. Data moves between devices by JAX's collectives and lax.ppermute only.
A program may use at most 128 MiB of HBM per device.

v0:
```python
import jax
import jax.numpy as jnp
from jax import lax
from jax.sharding import PartitionSpec as P

PANELS = 2


def contract_rows(gains, rows):
    return lax.dot_general(
        gains,
        rows,
        (((0,), (0,)), ((), ())),
        precision=lax.Precision.HIGHEST,
        preferred_element_type=jnp.float32,
    )


def solve_pivot(factor, rhs):
    half = lax.linalg.triangular_solve(factor, rhs, left_side=True, lower=True)
    return lax.linalg.triangular_solve(factor, half, left_side=True, lower=True, transpose_a=True)


def locate(listed, start, count):
    local_ids = listed - start
    valid = (local_ids >= 0) & (local_ids < count)
    clipped = jnp.clip(local_ids, 0, count - 1)
    marked = jnp.zeros((count,), jnp.float32).at[clipped].max(valid.astype(jnp.float32)) > 0.5
    return (clipped, valid, marked)


def per_device(hessian_inverse, weight, pruned):
    row_count = hessian_inverse.shape[0]
    col_count = hessian_inverse.shape[1]
    row_start = lax.axis_index("row") * row_count
    col_start = lax.axis_index("col") * col_count
    inverse = hessian_inverse
    slab = weight.astype(jnp.float32)
    for panel in range(PANELS):
        listed = pruned[panel]
        row_pick, row_valid, row_marked = locate(listed, row_start, row_count)
        col_pick, col_valid, col_marked = locate(listed, col_start, col_count)
        mine_rows = jnp.where(row_valid[:, None], jnp.take(inverse, row_pick, axis=0), 0.0)
        mine_slab = jnp.where(row_valid[:, None], jnp.take(slab, row_pick, axis=0), 0.0)
        panel_rows, slab_rows = lax.psum((mine_rows, mine_slab), "row")
        panel_pivot = jnp.where(col_valid[None, :], jnp.take(panel_rows, col_pick, axis=1), 0.0)
        pivot = lax.psum(panel_pivot, "col")
        factor = jnp.linalg.cholesky(pivot)
        mine_cols = jnp.where(col_valid[None, :], jnp.take(inverse, col_pick, axis=1), 0.0)
        columns = lax.psum(mine_cols, "col")
        gains = solve_pivot(factor, columns.T)
        slab = slab - contract_rows(gains, slab_rows)
        slab = jnp.where(row_marked[:, None], 0.0, slab)
        inverse = inverse - contract_rows(gains, panel_rows)
        inverse = jnp.where(row_marked[:, None] | col_marked[None, :], 0.0, inverse)
    return (inverse, slab.astype(jnp.bfloat16))


def solution(mesh):
    in_specs = (P("row", "col"), P("row", "col"), P())
    out_specs = (P("row", "col"), P("row", "col"))
    return jax.shard_map(
        per_device, mesh=mesh, in_specs=in_specs, out_specs=out_specs, check_vma=False
    )
```

profile of v0, /device:TPU:1, one launch (start us, length us, event | category | flops | bytes accessed | tf_op | source)
XLA Modules:
  0.0 719.2 jit_solution(886581179572580454)
XLA Ops:
  10.1 4.8 gather_fusion
  14.9 2.2 gather_fusion.6
  19.7 6.0 copy.13
  25.7 6.0 gather_fusion.2
  31.7 2.1 fusion.1
  33.8 53.3 %all-reduce.16.cloned.1.call-done = (f32[512,768]{1,0:T(8,128)}, f32[512,256]{1,0:T(8,128)}) async-done(((f32[512,768]{1,0:T(8,128)}, f32[512,256]{1,0:T(8,128)}), (f32[512,768]{1,0:T(8,128)}, f32[512,256]{1,0:T(8,128)})) %all-reduce.16.cloned.1.call-update) | async-done | bytes 2097168 | tf_op jit(solution)/shard_map/psum | solution.py:45
  87.1 1.9 copy.11
  91.9 4.1 scatter_custom_fusion.3
  96.0 3.7 scatter_custom_fusion.2
  99.8 96.6 %all-reduce.12.cloned.1.call-done = (f32[512,1536]{1,0:T(8,128)}, f32[512,512]{0,1:T(8,128)}) async-done(((f32[512,1536]{1,0:T(8,128)}, f32[512,512]{0,1:T(8,128)}), (f32[512,1536]{1,0:T(8,128)}, f32[512,512]{0,1:T(8,128)})) %all-reduce.12.cloned.1.call-update) | async-done | bytes 4194320 | tf_op jit(solution)/shard_map/psum | solution.py:50
  198.3 11.7 %cholesky.286 = f32[128,128]{1,0:T(8,128)S(1)} custom-call(f32[128,128]{1,0:T(8,128)S(1)} %cholesky.426), custom_call_target="Cholesky" | custom-call | tf_op jit(solution)/shard_map/jit(cholesky)/cholesky | solution.py:48
  210.2 9.8 %custom-call.31 = f32[1,128,128]{1,2,0:T(8,128)S(1)} custom-call(f32[1,128,128]{2,1,0:T(8,128)S(1)} %get-tuple-element.100), custom_call_target="InvertDiagBlocksLowerTriangular" | custom-call | tf_op jit(solution)/shard_map/jit(cholesky)/cholesky | solution.py:48
  220.6 11.7 %cholesky.305 = f32[128,128]{1,0:T(8,128)S(1)} custom-call(f32[128,128]{1,0:T(8,128)S(1)} %cholesky.430), custom_call_target="Cholesky" | custom-call | tf_op jit(solution)/shard_map/jit(cholesky)/cholesky | solution.py:48
  232.4 10.2 %custom-call.32 = f32[1,128,128]{1,2,0:T(8,128)S(1)} custom-call(f32[1,128,128]{2,1,0:T(8,128)S(1)} %get-tuple-element.97), custom_call_target="InvertDiagBlocksLowerTriangular" | custom-call | tf_op jit(solution)/shard_map/jit(cholesky)/cholesky | solution.py:48
  243.2 11.7 %cholesky.326 = f32[128,128]{1,0:T(8,128)S(1)} custom-call(f32[128,128]{1,0:T(8,128)S(1)} %cholesky.435), custom_call_target="Cholesky" | custom-call | tf_op jit(solution)/shard_map/jit(cholesky)/cholesky | solution.py:48
  255.0 9.8 %custom-call.33 = f32[1,128,128]{1,2,0:T(8,128)S(1)} custom-call(f32[1,128,128]{2,1,0:T(8,128)S(1)} %get-tuple-element.94), custom_call_target="InvertDiagBlocksLowerTriangular" | custom-call | tf_op jit(solution)/shard_map/jit(cholesky)/cholesky | solution.py:48
  265.4 11.7 %cholesky.343 = f32[128,128]{1,0:T(8,128)S(1)} custom-call(f32[128,128]{1,0:T(8,128)S(1)} %convolution_subtract_fusion.19), custom_call_target="Cholesky" | custom-call | tf_op jit(solution)/shard_map/jit(cholesky)/cholesky | solution.py:48
  282.0 7.6 %while.8 = (s32[]{:T(128)}, f32[512,512]{1,0:T(8,128)S(1)}, s32[4,2]{0,1:T(2,128)S(1)}, f32[4,128,128]{2,1,0:T(8,128)S(1)}, s32[]{:T(128)}) while((s32[]{:T(128)}, f32[512,512]{1,0:T(8,128)S(1)}, s32[4,2]{0,1:T(2,128)S(1)}, f32[4,128,128]{2,1,0:T(8,128)S(1)}, s32[]{:T(128)}) %tuple.80), condition=%wide.while_cond.1, body=%wide.while_body.1.sunk | while | flops 2 | bytes 131189 | solution.py:21
  289.6 39.3 %custom-call.35 = f32[4,128,128]{1,2,0:T(8,128)S(1)} custom-call(f32[4,128,128]{2,1,0:T(8,128)S(1)} %get-tuple-element.38), custom_call_target="InvertDiagBlocksLowerTriangular" | custom-call | tf_op jit(solution)/shard_map/triangular_solve/custom-call.8 | solution.py:21
  328.9 2.0 fusion.41
  330.9 2.1 convolution_subtract_fusion.13
  342.4 2.0 convolution_subtract_fusion.10
  345.3 10.7 %subtract_select_fusion.1 = f32[1536,768]{1,0:T(8,128)} fusion(f32[1536,768]{1,0:T(8,128)S(1)} %bitcast.167, f32[512,768]{1,0:T(8,128)S(1)} %copy-done.2, pred[768]{0:T(1024)(128)(4,1)S(1)} %broadcast_compare_fusion.2, pred[1536]{0:T(1024)(128)(4,1)S(1)} %broadcast_compare_fusion, f32[128,1536]{1,0:T(8,128)S(1)} %fusion.83, f32[128,1536]{1,0:T(8,128)S(1)} %fusion.81, ...), kind=kOutput, calls=%fused_computation.17 | convolution fusion | flops 7253655552 | bytes 14158080 | tf_op jit(solution)/shard_map/dot_general | solution.py:10
  356.0 5.5 fusion.3
  361.5 5.4 gather_fusion.3
  366.9 2.2 gather_fusion.7
  371.6 6.0 copy.16
  377.7 6.0 gather_fusion.5
  383.7 2.1 fusion
  385.8 50.2 %all-reduce.14.cloned.1.call-done = (f32[512,768]{1,0:T(8,128)}, f32[512,256]{1,0:T(8,128)}) async-done(((f32[512,768]{1,0:T(8,128)}, f32[512,256]{1,0:T(8,128)}), (f32[512,768]{1,0:T(8,128)}, f32[512,256]{1,0:T(8,128)})) %all-reduce.14.cloned.1.call-update) | async-done | bytes 2097168 | tf_op jit(solution)/shard_map/psum | solution.py:45
  436.0 1.9 copy.14
  440.7 4.1 scatter_custom_fusion.1
  444.8 3.7 scatter_custom_fusion
  448.5 96.7 %all-reduce.10.cloned.1.call-done = (f32[512,1536]{1,0:T(8,128)}, f32[512,512]{0,1:T(8,128)}) async-done(((f32[512,1536]{1,0:T(8,128)}, f32[512,512]{0,1:T(8,128)}), (f32[512,1536]{1,0:T(8,128)}, f32[512,512]{0,1:T(8,128)})) %all-reduce.10.cloned.1.call-update) | async-done | bytes 4194320 | tf_op jit(solution)/shard_map/psum | solution.py:50
  547.2 11.7 %cholesky.358 = f32[128,128]{1,0:T(8,128)S(1)} custom-call(f32[128,128]{1,0:T(8,128)S(1)} %cholesky.439), custom_call_target="Cholesky" | custom-call | tf_op jit(solution)/shard_map/jit(cholesky)/cholesky | solution.py:48
  559.0 9.8 %custom-call.36 = f32[1,128,128]{1,2,0:T(8,128)S(1)} custom-call(f32[1,128,128]{2,1,0:T(8,128)S(1)} %get-tuple-element.90), custom_call_target="InvertDiagBlocksLowerTriangular" | custom-call | tf_op jit(solution)/shard_map/jit(cholesky)/cholesky | solution.py:48
  569.5 11.7 %cholesky.377 = f32[128,128]{1,0:T(8,128)S(1)} custom-call(f32[128,128]{1,0:T(8,128)S(1)} %cholesky.443), custom_call_target="Cholesky" | custom-call | tf_op jit(solution)/shard_map/jit(cholesky)/cholesky | solution.py:48
  581.3 10.2 %custom-call.37 = f32[1,128,128]{1,2,0:T(8,128)S(1)} custom-call(f32[1,128,128]{2,1,0:T(8,128)S(1)} %get-tuple-element.87), custom_call_target="InvertDiagBlocksLowerTriangular" | custom-call | tf_op jit(solution)/shard_map/jit(cholesky)/cholesky | solution.py:48
  592.1 11.7 %cholesky.398 = f32[128,128]{1,0:T(8,128)S(1)} custom-call(f32[128,128]{1,0:T(8,128)S(1)} %cholesky.448), custom_call_target="Cholesky" | custom-call | tf_op jit(solution)/shard_map/jit(cholesky)/cholesky | solution.py:48
  603.9 9.8 %custom-call.38 = f32[1,128,128]{1,2,0:T(8,128)S(1)} custom-call(f32[1,128,128]{2,1,0:T(8,128)S(1)} %get-tuple-element.84), custom_call_target="InvertDiagBlocksLowerTriangular" | custom-call | tf_op jit(solution)/shard_map/jit(cholesky)/cholesky | solution.py:48
  614.3 11.7 %cholesky.415 = f32[128,128]{1,0:T(8,128)S(1)} custom-call(f32[128,128]{1,0:T(8,128)S(1)} %convolution_subtract_fusion.18), custom_call_target="Cholesky" | custom-call | tf_op jit(solution)/shard_map/jit(cholesky)/cholesky | solution.py:48
  631.7 8.1 %while.9 = (s32[]{:T(128)}, f32[512,512]{1,0:T(8,128)S(1)}, s32[4,2]{0,1:T(2,128)S(1)}, f32[4,128,128]{2,1,0:T(8,128)S(1)}, s32[]{:T(128)}) while((s32[]{:T(128)}, f32[512,512]{1,0:T(8,128)S(1)}, s32[4,2]{0,1:T(2,128)S(1)}, f32[4,128,128]{2,1,0:T(8,128)S(1)}, s32[]{:T(128)}) %tuple.98), condition=%wide.while_cond.1.clone, body=%wide.while_body.1.clone.sunk | while | flops 2 | bytes 131189 | solution.py:21
  639.8 39.3 %custom-call.40 = f32[4,128,128]{1,2,0:T(8,128)S(1)} custom-call(f32[4,128,128]{2,1,0:T(8,128)S(1)} %get-tuple-element.40), custom_call_target="InvertDiagBlocksLowerTriangular" | custom-call | tf_op jit(solution)/shard_map/triangular_solve/custom-call.8 | solution.py:21
  679.1 2.0 fusion.39
  681.1 2.1 convolution_subtract_fusion.9
  692.6 1.8 convolution_subtract_fusion.6
  695.3 10.7 %subtract_select_fusion = f32[1536,768]{1,0:T(8,128)} fusion(f32[1536,768]{1,0:T(8,128)S(1)} %bitcast.165, f32[512,768]{1,0:T(8,128)S(1)} %copy-done.3, pred[768]{0:T(1024)(128)(4,1)S(1)} %broadcast_compare_fusion.3, pred[1536]{0:T(1024)(128)(4,1)S(1)} %broadcast_compare_fusion.1, f32[128,1536]{1,0:T(8,128)S(1)} %fusion.90, f32[128,1536]{1,0:T(8,128)S(1)} %fusion.88, ...), kind=kOutput, calls=%fused_computation.16 | convolution fusion | flops 7253655552 | bytes 14158080 | tf_op jit(solution)/shard_map/dot_general | solution.py:10
  705.9 6.5 fusion.4
  (166 shorter events, 62.7 us)
Async XLA Ops:
  7.2 79.9 %all-reduce.16.cloned.1.call-start = ((), (), s32[]{:S(2)}) async-start(), calls=%async_computation.3 | async-start | bytes 4194304 | tf_op jit(solution)/shard_map/psum | solution.py:45
  17.2 1.4 copy-start.8
  19.6 176.8 %all-reduce.12.cloned.1.call-start = ((), (), s32[]{:S(2)}) async-start(), calls=%async_computation.1 | async-start | bytes 8388608 | tf_op jit(solution)/shard_map/psum | solution.py:50
  91.8 344.2 %all-reduce.14.cloned.1.call-start = ((), (), s32[]{:S(2)}) async-start(), calls=%async_computation.2 | async-start | bytes 4194304 | tf_op jit(solution)/shard_map/psum | solution.py:45
  196.4 1.7 copy-start.4
  330.9 2.9 copy-start.6
  338.2 7.0 slice-start.2
  340.6 4.6 slice-start.3
  342.4 2.8 copy-start.2
  345.2 10.7 %copy-start.10 = (bf16[1536,256]{1,0:T(8,128)(2,1)S(1)}, bf16[1536,256]{1,0:T(8,128)(2,1)}, u32[]{:S(2)}) copy-start(bf16[1536,256]{1,0:T(8,128)(2,1)} %param.17) | copy-start | bytes 2359300
  345.3 10.7 %copy-start.11 = (f32[512,256]{1,0:T(8,128)S(1)}, f32[512,256]{1,0:T(8,128)}, u32[]{:S(2)}) copy-start(f32[512,256]{1,0:T(8,128)} %get-tuple-element.68) | copy-start | bytes 1572868
  361.5 5.4 copy-start
  369.1 1.4 copy-start.9
  371.5 173.7 %all-reduce.10.cloned.1.call-start = ((), (), s32[]{:S(2)}) async-start(), calls=%async_computation | async-start | bytes 8388608 | tf_op jit(solution)/shard_map/psum | solution.py:50
  545.2 1.7 copy-start.5
  681.1 2.9 copy-start.7
  688.3 6.9 slice-start
  690.8 4.4 slice-start.1
  692.6 2.6 copy-start.3
  695.2 10.7 %copy-start.1 = (f32[1536,256]{1,0:T(8,128)S(1)}, f32[1536,256]{1,0:T(8,128)}, u32[]{:S(2)}) copy-start(f32[1536,256]{1,0:T(8,128)} %copy-done) | copy-start | bytes 4718596
  695.3 10.7 %copy-start.12 = (f32[512,256]{1,0:T(8,128)S(1)}, f32[512,256]{1,0:T(8,128)}, u32[]{:S(2)}) copy-start(f32[512,256]{1,0:T(8,128)} %get-tuple-element.66) | copy-start | bytes 1572868
Sparse Core Ops, SparseCore 0:
  19.7 67.3 all-reduce.15
  92.0 104.3 all-reduce.11
  371.7 64.2 all-reduce.13
  440.8 104.3 all-reduce.9
where the time goes:
time: 726 us; the launch traced here: 719 us
  waiting for transfers between devices  297 us (41%)
  other arithmetic  268 us (37%)
  matrix products  69.1 us (10%)
  local copies, waits for them, and re-layouts  65 us (9%)
  between operations  20.1 us (3%)
    psum x2, waiting for transfers between devices, per_device(): columns = lax.psum(mine_cols, 'col')  193 us
    another operation x29, other arithmetic, per_device(): factor = jnp.linalg.cholesky(pivot)  158 us
    psum x2, waiting for transfers between devices, per_device(): panel_rows, slab_rows = lax.psum((mine_rows, mine_slab), 'row')  104 us
    another operation x5, other arithmetic, solve_pivot(): lax.linalg.triangular_solve(factor, half, left_side=True, lower=True, tra...  79.2 us
    dot_general x4, matrix products, contract_rows(): lax.dot_general(gains, rows, (((0,), (0,)), ((), ())), precision=lax.Prec...  33.4 us
    another operation x14, matrix products, solve_pivot(): half = lax.linalg.triangular_solve(factor, rhs, left_side=True, lower=True)  18.3 us
    another operation x27, local copies, waits for them, and re-layouts, solve_pivot(): lax.linalg.triangular_solve(factor, half, left_side=True, lower=True, tra...  15.6 us
    another operation x4, other arithmetic, locate(): jnp.zeros((count,), jnp.float32).at[clipped].max(valid.astype(jnp.float32))  15.5 us
  transfers between devices with their start and end apart: 4, of which 4 were waited for; matrix products, arithmetic and copies ran while one was open for 6% of the time, Pallas kernels for 0%

commit v1 on v0

--- a/solution.py
+++ b/solution.py
@@ -47,7 +47,7 @@
         pivot = lax.psum(panel_pivot, "col")
         factor = jnp.linalg.cholesky(pivot)
         mine_cols = jnp.where(col_valid[None, :], jnp.take(inverse, col_pick, axis=1), 0.0)
-        columns = lax.psum(mine_cols, "col")
+        columns = jnp.sum(lax.all_gather(mine_cols, "col"), axis=0)
         gains = solve_pivot(factor, columns.T)
         slab = slab - contract_rows(gains, slab_rows)
         slab = jnp.where(row_marked[:, None], 0.0, slab)

time: 726 us -> 1130 us (1.56)
  waiting for transfers between devices: 297 us -> 567 us
  local copies, waits for them, and re-layouts: 65 us -> 171 us
  other arithmetic: 268 us -> 302 us
    all_gather x0 -> x2, waiting for transfers between devices: none -> 305 us  [per_device(): columns = jnp.sum(lax.all_gather(mine_cols, 'col'), axis=0)]
    unnamed x35 -> x33, local copies, waits for them, and re-layouts: 6.13 us -> 112 us
    psum x2, waiting for transfers between devices: 193 us -> 130 us  [per_device(): pivot = lax.psum(panel_pivot, 'col')]
    reduce_sum x0 -> x2, other arithmetic: none -> 34.5 us  [per_device(): columns = jnp.sum(lax.all_gather(mine_cols, 'col'), axis=0)]
    psum x2, waiting for transfers between devices: 104 us -> 132 us  [per_device(): panel_rows, slab_rows = lax.psum((mine_rows, mine_slab), 'row')]
  transfers between devices with their start and end apart: 4 -> 6, of which waited for: 4 -> 6; matrix products, arithmetic and copies ran while one was open for 6% -> 27% of each run, Pallas kernels for 0% -> 0%
where the time goes in v1:
time: 1130 us
  waiting for transfers between devices  567 us (50%)
  other arithmetic  302 us (27%)
  local copies, waits for them, and re-layouts  171 us (15%)
  matrix products  64.2 us (6%)
  between operations  20.4 us (2%)
    all_gather x2, waiting for transfers between devices, per_device(): columns = jnp.sum(lax.all_gather(mine_cols, 'col'), axis=0)  305 us
    another operation x29, other arithmetic, per_device(): factor = jnp.linalg.cholesky(pivot)  158 us
    psum x2, waiting for transfers between devices, per_device(): panel_rows, slab_rows = lax.psum((mine_rows, mine_slab), 'row')  132 us
    psum x2, waiting for transfers between devices, per_device(): pivot = lax.psum(panel_pivot, 'col')  130 us
    unnamed x33, local copies, waits for them, and re-layouts  112 us
    another operation x5, other arithmetic, solve_pivot(): lax.linalg.triangular_solve(factor, half, left_side=True, lower=True, tra...  79.3 us
    reduce_sum x2, other arithmetic, per_device(): columns = jnp.sum(lax.all_gather(mine_cols, 'col'), axis=0)  34.5 us
    dot_general x4, matrix products, contract_rows(): lax.dot_general(gains, rows, (((0,), (0,)), ((), ())), precision=lax.Prec...  33.4 us
  transfers between devices with their start and end apart: 6, of which 6 were waited for; matrix products, arithmetic and copies ran while one was open for 27% of the time, Pallas kernels for 0%

profile of v1, /device:TPU:1, one launch (start us, length us, event | category | flops | bytes accessed | tf_op | source)
XLA Modules:
  0.0 1125.6 jit_solution(4561291569028599523)
XLA Ops:
  10.1 4.8 gather_fusion
  14.9 2.2 gather_fusion.6
  19.7 67.4 %all-reduce.14.cloned.1.call-done = (f32[512,768]{1,0:T(8,128)}, f32[512,256]{1,0:T(8,128)}) async-done(((f32[512,768]{1,0:T(8,128)}, f32[512,256]{1,0:T(8,128)}), (f32[512,768]{1,0:T(8,128)}, f32[512,256]{1,0:T(8,128)})) %all-reduce.14.cloned.1.call-update) | async-done | bytes 2097168 | tf_op jit(solution)/shard_map/psum | solution.py:45
  87.1 1.9 copy.17
  91.9 6.0 copy.19
  97.9 6.0 gather_fusion.2
  104.0 2.1 bitcast_select_fusion.1
  106.1 4.1 scatter_custom_fusion.3
  110.2 4.0 scatter_custom_fusion.2
  114.3 64.7 %all-reduce.8.cloned.1.call-done = f32[512,512]{0,1:T(8,128)} async-done(((f32[512,512]{0,1:T(8,128)}), f32[512,512]{0,1:T(8,128)}) %all-reduce.8.cloned.1.call-update) | async-done | bytes 1048592 | tf_op jit(solution)/shard_map/psum | solution.py:47
  180.9 11.7 %cholesky.286 = f32[128,128]{1,0:T(8,128)S(1)} custom-call(f32[128,128]{1,0:T(8,128)S(1)} %cholesky.426), custom_call_target="Cholesky" | custom-call | tf_op jit(solution)/shard_map/jit(cholesky)/cholesky | solution.py:48
  192.8 9.8 custom-call.31
  203.2 11.7 %cholesky.305 = f32[128,128]{1,0:T(8,128)S(1)} custom-call(f32[128,128]{1,0:T(8,128)S(1)} %cholesky.430), custom_call_target="Cholesky" | custom-call | tf_op jit(solution)/shard_map/jit(cholesky)/cholesky | solution.py:48
  215.0 10.0 custom-call.32
  225.6 11.7 %cholesky.326 = f32[128,128]{1,0:T(8,128)S(1)} custom-call(f32[128,128]{1,0:T(8,128)S(1)} %cholesky.435), custom_call_target="Cholesky" | custom-call | tf_op jit(solution)/shard_map/jit(cholesky)/cholesky | solution.py:48
  237.4 9.8 custom-call.33
  247.8 11.7 %cholesky.343 = f32[128,128]{1,0:T(8,128)S(1)} custom-call(f32[128,128]{1,0:T(8,128)S(1)} %convolution_subtract_fusion.19), custom_call_target="Cholesky" | custom-call | tf_op jit(solution)/shard_map/jit(cholesky)/cholesky | solution.py:48
  264.6 8.4 while.8
  273.0 39.3 %custom-call.35 = f32[4,128,128]{1,2,0:T(8,128)S(1)} custom-call(f32[4,128,128]{2,1,0:T(8,128)S(1)} %get-tuple-element.38), custom_call_target="InvertDiagBlocksLowerTriangular" | custom-call | tf_op jit(solution)/shard_map/triangular_solve/custom-call.8 | solution.py:21
  312.3 153.1 %all-gather.5.cloned.1.call-done = f32[24576,512]{0,1:T(8,128)} async-done(((f32[1536,512]{0,1:T(8,128)}), f32[24576,512]{0,1:T(8,128)}) %all-gather.5.cloned.1.call-update) | async-done | bytes 50331664 | tf_op jit(solution)/shard_map/all_gather | solution.py:50
  465.4 53.0 %copy.23 = f32[64,8,16,1536]{3,2,1,0:T(8,128)} copy(f32[64,8,16,1536]{3,1,2,0:T(8,128)} %bitcast.172) | data formatting | bytes 100663296
  518.5 17.3 %bitcast_reduce_fusion.1 = f32[1536,512]{0,1:T(8,128)S(1)} fusion(f32[64,8,16,1536]{3,2,1,0:T(8,128)} %copy.23), kind=kLoop, calls=%fused_computation.17 | loop fusion | flops 11796480 | bytes 53477376 | tf_op jit(solution)/shard_map/reduce_sum | solution.py:50
  546.8 1.9 convolution_subtract_fusion.10
  549.6 10.7 subtract_select_fusion.1
  560.3 5.5 fusion.1
  565.8 5.4 gather_fusion.3
  571.2 2.2 gather_fusion.7
  576.0 64.2 %all-reduce.12.cloned.1.call-done = (f32[512,768]{1,0:T(8,128)}, f32[512,256]{1,0:T(8,128)}) async-done(((f32[512,768]{1,0:T(8,128)}, f32[512,256]{1,0:T(8,128)}), (f32[512,768]{1,0:T(8,128)}, f32[512,256]{1,0:T(8,128)})) %all-reduce.12.cloned.1.call-update) | async-done | bytes 2097168 | tf_op jit(solution)/shard_map/psum | solution.py:45
  644.9 6.0 copy.22
  650.9 6.0 gather_fusion.5
  656.9 2.0 bitcast_select_fusion
  659.0 4.1 scatter_custom_fusion.1
  663.1 3.9 scatter_custom_fusion
  667.0 65.0 %all-reduce.10.cloned.1.call-done = f32[512,512]{0,1:T(8,128)} async-done(((f32[512,512]{0,1:T(8,128)}), f32[512,512]{0,1:T(8,128)}) %all-reduce.10.cloned.1.call-update) | async-done | bytes 1048592 | tf_op jit(solution)/shard_map/psum | solution.py:47
  733.9 11.7 %cholesky.358 = f32[128,128]{1,0:T(8,128)S(1)} custom-call(f32[128,128]{1,0:T(8,128)S(1)} %cholesky.439), custom_call_target="Cholesky" | custom-call | tf_op jit(solution)/shard_map/jit(cholesky)/cholesky | solution.py:48
  745.8 9.8 custom-call.36
  756.2 11.7 %cholesky.377 = f32[128,128]{1,0:T(8,128)S(1)} custom-call(f32[128,128]{1,0:T(8,128)S(1)} %cholesky.443), custom_call_target="Cholesky" | custom-call | tf_op jit(solution)/shard_map/jit(cholesky)/cholesky | solution.py:48
  768.0 10.0 custom-call.37
  778.6 11.7 %cholesky.398 = f32[128,128]{1,0:T(8,128)S(1)} custom-call(f32[128,128]{1,0:T(8,128)S(1)} %cholesky.448), custom_call_target="Cholesky" | custom-call | tf_op jit(solution)/shard_map/jit(cholesky)/cholesky | solution.py:48
  790.4 9.8 custom-call.38
  800.8 11.7 %cholesky.415 = f32[128,128]{1,0:T(8,128)S(1)} custom-call(f32[128,128]{1,0:T(8,128)S(1)} %convolution_subtract_fusion.18), custom_call_target="Cholesky" | custom-call | tf_op jit(solution)/shard_map/jit(cholesky)/cholesky | solution.py:48
  818.0 7.7 while.9
  825.8 39.3 %custom-call.40 = f32[4,128,128]{1,2,0:T(8,128)S(1)} custom-call(f32[4,128,128]{2,1,0:T(8,128)S(1)} %get-tuple-element.40), custom_call_target="InvertDiagBlocksLowerTriangular" | custom-call | tf_op jit(solution)/shard_map/triangular_solve/custom-call.8 | solution.py:21
  865.1 152.3 %all-gather.7.cloned.1.call-done = f32[24576,512]{0,1:T(8,128)} async-done(((f32[1536,512]{0,1:T(8,128)}), f32[24576,512]{0,1:T(8,128)}) %all-gather.7.cloned.1.call-update) | async-done | bytes 50331664 | tf_op jit(solution)/shard_map/all_gather | solution.py:50
  1017.4 53.0 %copy.24 = f32[64,8,16,1536]{3,2,1,0:T(8,128)} copy(f32[64,8,16,1536]{3,1,2,0:T(8,128)} %bitcast.173) | data formatting | bytes 100663296
  1070.4 17.2 %bitcast_reduce_fusion = f32[1536,512]{0,1:T(8,128)S(1)} fusion(f32[64,8,16,1536]{3,2,1,0:T(8,128)} %copy.24), kind=kLoop, calls=%fused_computation.16 | loop fusion | flops 11796480 | bytes 53477376 | tf_op jit(solution)/shard_map/reduce_sum | solution.py:50
  1101.3 10.7 subtract_select_fusion
  1112.0 6.6 fusion.2
  (172 shorter events, 70.1 us)
Async XLA Ops:
  7.2 79.9 %all-reduce.14.cloned.1.call-start = ((), (), s32[]{:S(2)}) async-start(), calls=%async_computation.5 | async-start | bytes 4194304 | tf_op jit(solution)/shard_map/psum | solution.py:45
  17.2 1.4 copy-start.6
  19.6 159.4 %all-reduce.8.cloned.1.call-start = ((), (), s32[]{:S(2)}) async-start(), calls=%async_computation | async-start | bytes 2097152 | tf_op jit(solution)/shard_map/psum | solution.py:47
  91.8 373.6 %all-gather.5.cloned.1.call-start = ((), (), s32[]{:S(2)}) async-start(), calls=%async_computation.2 | async-start | bytes 53477376 | tf_op jit(solution)/shard_map/all_gather | solution.py:50
  106.0 534.1 %all-reduce.12.cloned.1.call-start = ((), (), s32[]{:S(2)}) async-start(), calls=%async_computation.4 | async-start | bytes 4194304 | tf_op jit(solution)/shard_map/psum | solution.py:45
  179.0 1.7 copy-start.4
  541.7 7.9 slice-start.2
  545.0 4.6 slice-start.3
  546.8 2.8 copy-start.2
  549.6 10.7 copy-start.8
  549.6 10.7 copy-start.9
  565.8 5.4 copy-start
  573.5 1.4 copy-start.7
  575.9 156.1 %all-reduce.10.cloned.1.call-start = ((), (), s32[]{:S(2)}) async-start(), calls=%async_computation.1 | async-start | bytes 2097152 | tf_op jit(solution)/shard_map/psum | solution.py:47
  644.8 372.5 %all-gather.7.cloned.1.call-start = ((), (), s32[]{:S(2)}) async-start(), calls=%async_computation.3 | async-start | bytes 53477376 | tf_op jit(solution)/shard_map/all_gather | solution.py:50
  732.0 1.7 copy-start.5
  1093.6 7.7 slice-start
  1096.9 4.4 slice-start.1
  1098.7 2.6 copy-start.3
  1101.3 10.7 copy-start.1
  1101.3 10.7 copy-start.10
Sparse Core Ops, SparseCore 0:
  19.7 67.3 all-reduce.13
  92.0 86.9 all-reduce.7
  181.7 283.6 all-gather.4
  576.0 64.0 all-reduce.11
  645.0 86.9 all-reduce.9
  734.0 283.3 all-gather.6
